TPU v7x, 128 devices: a whole 4x4x4 slice. The times are simulated.
128 devices in a mesh: rows: 16 (over z, x), feat: 8 (over y, core).
Axes of the slice: x: 4, y: 4, z: 4, core: 2. Of those that a mesh axis runs over, the one named last changes fastest.
Arguments:
- scores: float32 [524288, 64], P(('rows', 'feat'))
- labels: int32 [524288], P('rows'), may hold values from 0 to 63
- bins: int32 [256, 524288], P('feat', 'rows'), may hold values from 0 to 63
- elected: int32 [64, 32], P(None, 'feat'), may hold values from 0 to 255, as said below
Outputs:
- gains: float32 [64, 32, 63], P('rows', 'feat')
Inputs may be any that keep to these rules, and one draw needn't show every extreme that they name: `elected`: for every class and every j < 8, columns j * 4 to (j + 1) * 4 - 1 hold 4 distinct features of the range j * 32 to (j + 1) * 32 - 1.
All inputs are finite; a program needn't handle non-finite values.
Results may differ from a plain program's by a relative error of at most 0.0026.
Values may be sent and summed in bfloat16 or wider, within the bound.
A program may use at most 64 MiB of HBM per device.

v0:
```python
import math

import jax
import jax.numpy as jnp
from jax import lax
from jax.sharding import PartitionSpec as P

BINS = 64


l2_penalty = 1.0


def in_blocks(value, dim, size):
    before, after = (value.shape[:dim], value.shape[dim + 1 :])
    return jnp.moveaxis(value.reshape(*before, size, -1, *after), dim, 0)


def sum_at_owner(value, axis, dim):
    size = lax.axis_size(axis)
    blocks = lax.all_to_all(in_blocks(value, dim, size), axis, 0, 0, tiled=True)
    return jnp.sum(blocks, axis=0)


def grad_columns(scores, labels):
    row_max = jnp.max(scores, axis=1, keepdims=True)
    expon = jnp.exp(scores - row_max)
    probs = expon / jnp.sum(expon, axis=1, keepdims=True)
    target = (labels[:, None] == jnp.arange(scores.shape[1], dtype=jnp.int32)[None, :]).astype(
        jnp.float32
    )
    grad = (probs - target).astype(jnp.bfloat16)
    hess = (probs * (1.0 - probs)).astype(jnp.bfloat16)
    return jnp.concatenate([grad, hess], axis=1)


def split_gains(hist):
    left_g = jnp.cumsum(hist[..., 0], axis=-1)
    left_h = jnp.cumsum(hist[..., 1], axis=-1)
    tot_g = left_g[..., -1:]
    tot_h = left_h[..., -1:]
    right_g = tot_g - left_g
    right_h = tot_h - left_h
    split_gain = 0.5 * (
        left_g * left_g / (left_h + l2_penalty)
        + right_g * right_g / (right_h + l2_penalty)
        - tot_g * tot_g / (tot_h + l2_penalty)
    )
    return split_gain[..., :-1]


def shards(scores, labels, bins, elected):
    feat_group = bins.shape[0]
    own_rows = scores.shape[0]
    classes = scores.shape[1]
    bin_ids = jnp.arange(BINS, dtype=jnp.int32)
    empty = jnp.zeros((feat_group * BINS, 2 * classes), jnp.float32)
    own_labels = lax.dynamic_slice_in_dim(labels, lax.axis_index("feat") * own_rows, own_rows, 0)
    grad_hess = grad_columns(scores, own_labels)
    grad_rows = lax.all_gather(grad_hess, "feat", axis=0, tiled=True)
    piece_rows = grad_rows.shape[0]
    block_len = math.gcd(piece_rows, 2048)

    def step(block_idx, acc):
        block_cols = lax.dynamic_slice_in_dim(grad_rows, block_idx * block_len, block_len, 0)
        bin_codes = lax.dynamic_slice_in_dim(bins, block_idx * block_len, block_len, 1)
        onehot = (bin_codes[:, None, :] == bin_ids[None, :, None]).astype(jnp.bfloat16)
        onehot = onehot.reshape(feat_group * BINS, block_len)
        return acc + jnp.dot(onehot, block_cols, preferred_element_type=jnp.float32)

    hist = lax.fori_loop(0, piece_rows // block_len, step, empty)
    hist_four = hist.reshape(feat_group, BINS, 2, classes)
    local_index = elected - lax.axis_index("feat") * feat_group
    selector = (
        local_index[:, :, None] == jnp.arange(feat_group, dtype=jnp.int32)[None, None, :]
    ).astype(jnp.float32)
    picked_all = jnp.einsum("cef,fbkc->cebk", selector, hist_four, precision=lax.Precision.HIGHEST)
    picked = sum_at_owner(picked_all, "rows", 0)
    return split_gains(picked)


def solution(mesh):
    return jax.shard_map(
        shards,
        mesh=mesh,
        in_specs=(P(("rows", "feat"), None), P("rows"), P("feat", "rows"), P(None, "feat")),
        out_specs=P("rows", "feat", None),
        check_vma=False,
    )
```

profile of v0, /device:TPU:0, one launch (start us, length us, event | category | flops | bytes accessed | tf_op | source)
XLA Modules:
  0.0 263.1 jit_solution(3021899708609091716)
XLA Ops:
  6.5 1.3 reduce_max.9
  7.8 1.4 fusion.6
  10.0 1.6 subtract_convert_fusion
  11.5 1.2 pad_maximum_fusion
  12.9 52.2 %all-gather.2.cloned.1.call-done = bf16[32768,128]{0,1:T(8,128)(2,1)} async-done(((bf16[4096,128]{0,1:T(8,128)(2,1)}), bf16[32768,128]{0,1:T(8,128)(2,1)}) %all-gather.2.cloned.1.call-update) | async-done | bytes 8388624 | tf_op jit(solution)/shard_map/all_gather | solution.py:60
  65.0 165.3 %while.14 = (s32[]{:T(128)}, f32[2048,128]{1,0:T(8,128)S(1)}, s32[32,32768]{1,0:T(8,128)}, bf16[32768,128]{0,1:T(8,128)(2,1)}, s32[]{:T(128)}, /*index=5*/s32[]{:T(128)}, s32[]{:T(128)}, s32[]{:T(128)}) while((s32[]{:T(128)}, f32[2048,128]{1,0:T(8,128)S(1)}, s32[32,32768]{1,0:T(8,128)}, bf16[32768,128]{0,1:T(8,128)(2,1)}, ...), condition=%wide.region_3.0_spmd.clone, body=%wide.region_2.0_spmd.clone.sunk | while | flops 1078460416 | bytes 11829397 | solution.py:71
  66.1 4.3 %bitcast_compare_fusion.2 = pred[2048,2048]{1,0:T(32,128)(4,1)} fusion(s32[2048]{0:T(1024)S(1)} %eq.103, s32[32,2048]{1,0:T(8,128)S(1)} %constant_dynamic-slice_fusion.2), kind=kLoop, calls=%fused_computation.1.clone.1 | loop fusion | flops 4194304 | bytes 4464640 | tf_op jit(solution)/shard_map/while/body/eval_jaxpr/eq | solution.py:67
  70.3 5.0 %convolution_add_fusion.2 = f32[2048,128]{1,0:T(8,128)S(1)} fusion(pred[2048,2048]{1,0:T(32,128)(4,1)} %bitcast_compare_fusion.2, f32[2048,128]{1,0:T(8,128)S(1)} %get-tuple-element.170, bf16[32768,128]{0,1:T(8,128)(2,1)} %get-tuple-element.180, s32[]{:T(128)S(6)} %select_n.14, pred[]{:T(512)S(6)} %compare.3), kind=kOutput, calls=%fused_computation.2.clone.1 | convolution fusion | flops 1074266112 | bytes 6815749 | tf_op jit(solution)/shard_map/while/body/eval_jaxpr/dot_general | solution.py:69
  75.4 1.0 constant_dynamic-slice_fusion.2
  76.4 4.3 %bitcast_compare_fusion.2 = pred[2048,2048]{1,0:T(32,128)(4,1)} fusion(s32[2048]{0:T(1024)S(1)} %eq.103, s32[32,2048]{1,0:T(8,128)S(1)} %constant_dynamic-slice_fusion.2), kind=kLoop, calls=%fused_computation.1.clone.1 | loop fusion | flops 4194304 | bytes 4464640 | tf_op jit(solution)/shard_map/while/body/eval_jaxpr/eq | solution.py:67
  80.7 5.0 %convolution_add_fusion.2 = f32[2048,128]{1,0:T(8,128)S(1)} fusion(pred[2048,2048]{1,0:T(32,128)(4,1)} %bitcast_compare_fusion.2, f32[2048,128]{1,0:T(8,128)S(1)} %get-tuple-element.170, bf16[32768,128]{0,1:T(8,128)(2,1)} %get-tuple-element.180, s32[]{:T(128)S(6)} %select_n.14, pred[]{:T(512)S(6)} %compare.3), kind=kOutput, calls=%fused_computation.2.clone.1 | convolution fusion | flops 1074266112 | bytes 6815749 | tf_op jit(solution)/shard_map/while/body/eval_jaxpr/dot_general | solution.py:69
  85.7 1.0 constant_dynamic-slice_fusion.2
  86.8 4.3 %bitcast_compare_fusion.2 = pred[2048,2048]{1,0:T(32,128)(4,1)} fusion(s32[2048]{0:T(1024)S(1)} %eq.103, s32[32,2048]{1,0:T(8,128)S(1)} %constant_dynamic-slice_fusion.2), kind=kLoop, calls=%fused_computation.1.clone.1 | loop fusion | flops 4194304 | bytes 4464640 | tf_op jit(solution)/shard_map/while/body/eval_jaxpr/eq | solution.py:67
  91.0 5.0 %convolution_add_fusion.2 = f32[2048,128]{1,0:T(8,128)S(1)} fusion(pred[2048,2048]{1,0:T(32,128)(4,1)} %bitcast_compare_fusion.2, f32[2048,128]{1,0:T(8,128)S(1)} %get-tuple-element.170, bf16[32768,128]{0,1:T(8,128)(2,1)} %get-tuple-element.180, s32[]{:T(128)S(6)} %select_n.14, pred[]{:T(512)S(6)} %compare.3), kind=kOutput, calls=%fused_computation.2.clone.1 | convolution fusion | flops 1074266112 | bytes 6815749 | tf_op jit(solution)/shard_map/while/body/eval_jaxpr/dot_general | solution.py:69
  96.0 1.0 constant_dynamic-slice_fusion.2
  97.1 4.3 %bitcast_compare_fusion.2 = pred[2048,2048]{1,0:T(32,128)(4,1)} fusion(s32[2048]{0:T(1024)S(1)} %eq.103, s32[32,2048]{1,0:T(8,128)S(1)} %constant_dynamic-slice_fusion.2), kind=kLoop, calls=%fused_computation.1.clone.1 | loop fusion | flops 4194304 | bytes 4464640 | tf_op jit(solution)/shard_map/while/body/eval_jaxpr/eq | solution.py:67
  101.3 5.0 %convolution_add_fusion.2 = f32[2048,128]{1,0:T(8,128)S(1)} fusion(pred[2048,2048]{1,0:T(32,128)(4,1)} %bitcast_compare_fusion.2, f32[2048,128]{1,0:T(8,128)S(1)} %get-tuple-element.170, bf16[32768,128]{0,1:T(8,128)(2,1)} %get-tuple-element.180, s32[]{:T(128)S(6)} %select_n.14, pred[]{:T(512)S(6)} %compare.3), kind=kOutput, calls=%fused_computation.2.clone.1 | convolution fusion | flops 1074266112 | bytes 6815749 | tf_op jit(solution)/shard_map/while/body/eval_jaxpr/dot_general | solution.py:69
  106.4 1.0 constant_dynamic-slice_fusion.2
  107.4 4.3 %bitcast_compare_fusion.2 = pred[2048,2048]{1,0:T(32,128)(4,1)} fusion(s32[2048]{0:T(1024)S(1)} %eq.103, s32[32,2048]{1,0:T(8,128)S(1)} %constant_dynamic-slice_fusion.2), kind=kLoop, calls=%fused_computation.1.clone.1 | loop fusion | flops 4194304 | bytes 4464640 | tf_op jit(solution)/shard_map/while/body/eval_jaxpr/eq | solution.py:67
  111.7 5.0 %convolution_add_fusion.2 = f32[2048,128]{1,0:T(8,128)S(1)} fusion(pred[2048,2048]{1,0:T(32,128)(4,1)} %bitcast_compare_fusion.2, f32[2048,128]{1,0:T(8,128)S(1)} %get-tuple-element.170, bf16[32768,128]{0,1:T(8,128)(2,1)} %get-tuple-element.180, s32[]{:T(128)S(6)} %select_n.14, pred[]{:T(512)S(6)} %compare.3), kind=kOutput, calls=%fused_computation.2.clone.1 | convolution fusion | flops 1074266112 | bytes 6815749 | tf_op jit(solution)/shard_map/while/body/eval_jaxpr/dot_general | solution.py:69
  116.7 1.0 constant_dynamic-slice_fusion.2
  117.8 4.3 %bitcast_compare_fusion.2 = pred[2048,2048]{1,0:T(32,128)(4,1)} fusion(s32[2048]{0:T(1024)S(1)} %eq.103, s32[32,2048]{1,0:T(8,128)S(1)} %constant_dynamic-slice_fusion.2), kind=kLoop, calls=%fused_computation.1.clone.1 | loop fusion | flops 4194304 | bytes 4464640 | tf_op jit(solution)/shard_map/while/body/eval_jaxpr/eq | solution.py:67
  122.0 5.0 %convolution_add_fusion.2 = f32[2048,128]{1,0:T(8,128)S(1)} fusion(pred[2048,2048]{1,0:T(32,128)(4,1)} %bitcast_compare_fusion.2, f32[2048,128]{1,0:T(8,128)S(1)} %get-tuple-element.170, bf16[32768,128]{0,1:T(8,128)(2,1)} %get-tuple-element.180, s32[]{:T(128)S(6)} %select_n.14, pred[]{:T(512)S(6)} %compare.3), kind=kOutput, calls=%fused_computation.2.clone.1 | convolution fusion | flops 1074266112 | bytes 6815749 | tf_op jit(solution)/shard_map/while/body/eval_jaxpr/dot_general | solution.py:69
  127.0 1.0 constant_dynamic-slice_fusion.2
  128.1 4.3 %bitcast_compare_fusion.2 = pred[2048,2048]{1,0:T(32,128)(4,1)} fusion(s32[2048]{0:T(1024)S(1)} %eq.103, s32[32,2048]{1,0:T(8,128)S(1)} %constant_dynamic-slice_fusion.2), kind=kLoop, calls=%fused_computation.1.clone.1 | loop fusion | flops 4194304 | bytes 4464640 | tf_op jit(solution)/shard_map/while/body/eval_jaxpr/eq | solution.py:67
  132.3 5.0 %convolution_add_fusion.2 = f32[2048,128]{1,0:T(8,128)S(1)} fusion(pred[2048,2048]{1,0:T(32,128)(4,1)} %bitcast_compare_fusion.2, f32[2048,128]{1,0:T(8,128)S(1)} %get-tuple-element.170, bf16[32768,128]{0,1:T(8,128)(2,1)} %get-tuple-element.180, s32[]{:T(128)S(6)} %select_n.14, pred[]{:T(512)S(6)} %compare.3), kind=kOutput, calls=%fused_computation.2.clone.1 | convolution fusion | flops 1074266112 | bytes 6815749 | tf_op jit(solution)/shard_map/while/body/eval_jaxpr/dot_general | solution.py:69
  138.4 4.3 %bitcast_compare_fusion.2 = pred[2048,2048]{1,0:T(32,128)(4,1)} fusion(s32[2048]{0:T(1024)S(1)} %eq.103, s32[32,2048]{1,0:T(8,128)S(1)} %constant_dynamic-slice_fusion.2), kind=kLoop, calls=%fused_computation.1.clone.1 | loop fusion | flops 4194304 | bytes 4464640 | tf_op jit(solution)/shard_map/while/body/eval_jaxpr/eq | solution.py:67
  142.7 5.0 %convolution_add_fusion.2 = f32[2048,128]{1,0:T(8,128)S(1)} fusion(pred[2048,2048]{1,0:T(32,128)(4,1)} %bitcast_compare_fusion.2, f32[2048,128]{1,0:T(8,128)S(1)} %get-tuple-element.170, bf16[32768,128]{0,1:T(8,128)(2,1)} %get-tuple-element.180, s32[]{:T(128)S(6)} %select_n.14, pred[]{:T(512)S(6)} %compare.3), kind=kOutput, calls=%fused_computation.2.clone.1 | convolution fusion | flops 1074266112 | bytes 6815749 | tf_op jit(solution)/shard_map/while/body/eval_jaxpr/dot_general | solution.py:69
  148.8 4.3 %bitcast_compare_fusion.2 = pred[2048,2048]{1,0:T(32,128)(4,1)} fusion(s32[2048]{0:T(1024)S(1)} %eq.103, s32[32,2048]{1,0:T(8,128)S(1)} %constant_dynamic-slice_fusion.2), kind=kLoop, calls=%fused_computation.1.clone.1 | loop fusion | flops 4194304 | bytes 4464640 | tf_op jit(solution)/shard_map/while/body/eval_jaxpr/eq | solution.py:67
  153.0 5.0 %convolution_add_fusion.2 = f32[2048,128]{1,0:T(8,128)S(1)} fusion(pred[2048,2048]{1,0:T(32,128)(4,1)} %bitcast_compare_fusion.2, f32[2048,128]{1,0:T(8,128)S(1)} %get-tuple-element.170, bf16[32768,128]{0,1:T(8,128)(2,1)} %get-tuple-element.180, s32[]{:T(128)S(6)} %select_n.14, pred[]{:T(512)S(6)} %compare.3), kind=kOutput, calls=%fused_computation.2.clone.1 | convolution fusion | flops 1074266112 | bytes 6815749 | tf_op jit(solution)/shard_map/while/body/eval_jaxpr/dot_general | solution.py:69
  159.1 4.3 %bitcast_compare_fusion.2 = pred[2048,2048]{1,0:T(32,128)(4,1)} fusion(s32[2048]{0:T(1024)S(1)} %eq.103, s32[32,2048]{1,0:T(8,128)S(1)} %constant_dynamic-slice_fusion.2), kind=kLoop, calls=%fused_computation.1.clone.1 | loop fusion | flops 4194304 | bytes 4464640 | tf_op jit(solution)/shard_map/while/body/eval_jaxpr/eq | solution.py:67
  163.3 5.0 %convolution_add_fusion.2 = f32[2048,128]{1,0:T(8,128)S(1)} fusion(pred[2048,2048]{1,0:T(32,128)(4,1)} %bitcast_compare_fusion.2, f32[2048,128]{1,0:T(8,128)S(1)} %get-tuple-element.170, bf16[32768,128]{0,1:T(8,128)(2,1)} %get-tuple-element.180, s32[]{:T(128)S(6)} %select_n.14, pred[]{:T(512)S(6)} %compare.3), kind=kOutput, calls=%fused_computation.2.clone.1 | convolution fusion | flops 1074266112 | bytes 6815749 | tf_op jit(solution)/shard_map/while/body/eval_jaxpr/dot_general | solution.py:69
  169.4 4.3 %bitcast_compare_fusion.2 = pred[2048,2048]{1,0:T(32,128)(4,1)} fusion(s32[2048]{0:T(1024)S(1)} %eq.103, s32[32,2048]{1,0:T(8,128)S(1)} %constant_dynamic-slice_fusion.2), kind=kLoop, calls=%fused_computation.1.clone.1 | loop fusion | flops 4194304 | bytes 4464640 | tf_op jit(solution)/shard_map/while/body/eval_jaxpr/eq | solution.py:67
  173.7 5.0 %convolution_add_fusion.2 = f32[2048,128]{1,0:T(8,128)S(1)} fusion(pred[2048,2048]{1,0:T(32,128)(4,1)} %bitcast_compare_fusion.2, f32[2048,128]{1,0:T(8,128)S(1)} %get-tuple-element.170, bf16[32768,128]{0,1:T(8,128)(2,1)} %get-tuple-element.180, s32[]{:T(128)S(6)} %select_n.14, pred[]{:T(512)S(6)} %compare.3), kind=kOutput, calls=%fused_computation.2.clone.1 | convolution fusion | flops 1074266112 | bytes 6815749 | tf_op jit(solution)/shard_map/while/body/eval_jaxpr/dot_general | solution.py:69
  178.7 1.0 constant_dynamic-slice_fusion.2
  179.8 4.3 %bitcast_compare_fusion.2 = pred[2048,2048]{1,0:T(32,128)(4,1)} fusion(s32[2048]{0:T(1024)S(1)} %eq.103, s32[32,2048]{1,0:T(8,128)S(1)} %constant_dynamic-slice_fusion.2), kind=kLoop, calls=%fused_computation.1.clone.1 | loop fusion | flops 4194304 | bytes 4464640 | tf_op jit(solution)/shard_map/while/body/eval_jaxpr/eq | solution.py:67
  184.0 5.0 %convolution_add_fusion.2 = f32[2048,128]{1,0:T(8,128)S(1)} fusion(pred[2048,2048]{1,0:T(32,128)(4,1)} %bitcast_compare_fusion.2, f32[2048,128]{1,0:T(8,128)S(1)} %get-tuple-element.170, bf16[32768,128]{0,1:T(8,128)(2,1)} %get-tuple-element.180, s32[]{:T(128)S(6)} %select_n.14, pred[]{:T(512)S(6)} %compare.3), kind=kOutput, calls=%fused_computation.2.clone.1 | convolution fusion | flops 1074266112 | bytes 6815749 | tf_op jit(solution)/shard_map/while/body/eval_jaxpr/dot_general | solution.py:69
  190.1 4.3 %bitcast_compare_fusion.2 = pred[2048,2048]{1,0:T(32,128)(4,1)} fusion(s32[2048]{0:T(1024)S(1)} %eq.103, s32[32,2048]{1,0:T(8,128)S(1)} %constant_dynamic-slice_fusion.2), kind=kLoop, calls=%fused_computation.1.clone.1 | loop fusion | flops 4194304 | bytes 4464640 | tf_op jit(solution)/shard_map/while/body/eval_jaxpr/eq | solution.py:67
  194.3 5.0 %convolution_add_fusion.2 = f32[2048,128]{1,0:T(8,128)S(1)} fusion(pred[2048,2048]{1,0:T(32,128)(4,1)} %bitcast_compare_fusion.2, f32[2048,128]{1,0:T(8,128)S(1)} %get-tuple-element.170, bf16[32768,128]{0,1:T(8,128)(2,1)} %get-tuple-element.180, s32[]{:T(128)S(6)} %select_n.14, pred[]{:T(512)S(6)} %compare.3), kind=kOutput, calls=%fused_computation.2.clone.1 | convolution fusion | flops 1074266112 | bytes 6815749 | tf_op jit(solution)/shard_map/while/body/eval_jaxpr/dot_general | solution.py:69
  200.4 4.3 %bitcast_compare_fusion.2 = pred[2048,2048]{1,0:T(32,128)(4,1)} fusion(s32[2048]{0:T(1024)S(1)} %eq.103, s32[32,2048]{1,0:T(8,128)S(1)} %constant_dynamic-slice_fusion.2), kind=kLoop, calls=%fused_computation.1.clone.1 | loop fusion | flops 4194304 | bytes 4464640 | tf_op jit(solution)/shard_map/while/body/eval_jaxpr/eq | solution.py:67
  204.7 5.0 %convolution_add_fusion.2 = f32[2048,128]{1,0:T(8,128)S(1)} fusion(pred[2048,2048]{1,0:T(32,128)(4,1)} %bitcast_compare_fusion.2, f32[2048,128]{1,0:T(8,128)S(1)} %get-tuple-element.170, bf16[32768,128]{0,1:T(8,128)(2,1)} %get-tuple-element.180, s32[]{:T(128)S(6)} %select_n.14, pred[]{:T(512)S(6)} %compare.3), kind=kOutput, calls=%fused_computation.2.clone.1 | convolution fusion | flops 1074266112 | bytes 6815749 | tf_op jit(solution)/shard_map/while/body/eval_jaxpr/dot_general | solution.py:69
  210.8 4.3 %bitcast_compare_fusion.2 = pred[2048,2048]{1,0:T(32,128)(4,1)} fusion(s32[2048]{0:T(1024)S(1)} %eq.103, s32[32,2048]{1,0:T(8,128)S(1)} %constant_dynamic-slice_fusion.2), kind=kLoop, calls=%fused_computation.1.clone.1 | loop fusion | flops 4194304 | bytes 4464640 | tf_op jit(solution)/shard_map/while/body/eval_jaxpr/eq | solution.py:67
  215.0 5.0 %convolution_add_fusion.2 = f32[2048,128]{1,0:T(8,128)S(1)} fusion(pred[2048,2048]{1,0:T(32,128)(4,1)} %bitcast_compare_fusion.2, f32[2048,128]{1,0:T(8,128)S(1)} %get-tuple-element.170, bf16[32768,128]{0,1:T(8,128)(2,1)} %get-tuple-element.180, s32[]{:T(128)S(6)} %select_n.14, pred[]{:T(512)S(6)} %compare.3), kind=kOutput, calls=%fused_computation.2.clone.1 | convolution fusion | flops 1074266112 | bytes 6815749 | tf_op jit(solution)/shard_map/while/body/eval_jaxpr/dot_general | solution.py:69
  221.1 4.3 %bitcast_compare_fusion.2 = pred[2048,2048]{1,0:T(32,128)(4,1)} fusion(s32[2048]{0:T(1024)S(1)} %eq.103, s32[32,2048]{1,0:T(8,128)S(1)} %constant_dynamic-slice_fusion.2), kind=kLoop, calls=%fused_computation.1.clone.1 | loop fusion | flops 4194304 | bytes 4464640 | tf_op jit(solution)/shard_map/while/body/eval_jaxpr/eq | solution.py:67
  225.3 5.0 %convolution_add_fusion.2 = f32[2048,128]{1,0:T(8,128)S(1)} fusion(pred[2048,2048]{1,0:T(32,128)(4,1)} %bitcast_compare_fusion.2, f32[2048,128]{1,0:T(8,128)S(1)} %get-tuple-element.170, bf16[32768,128]{0,1:T(8,128)(2,1)} %get-tuple-element.180, s32[]{:T(128)S(6)} %select_n.14, pred[]{:T(512)S(6)} %compare.3), kind=kOutput, calls=%fused_computation.2.clone.1 | convolution fusion | flops 1074266112 | bytes 6815749 | tf_op jit(solution)/shard_map/while/body/eval_jaxpr/dot_general | solution.py:69
  230.3 2.5 reshape.21
  232.9 3.1 %copy.16 = f32[32,64,2,64]{1,0,2,3:T(8,128)S(1)} copy(f32[32,64,2,64]{3,2,1,0:T(2,128)} %reshape.21) | data formatting | bytes 2097152 | tf_op jit(solution)/shard_map/reshape | solution.py:72
  237.0 14.7 %all_to_all.5 = f32[16,1,2048]{2,1,0:T(1,128)S(1)} all-to-all(f32[16,1,2048]{2,1,0:T(1,128)S(1)} %reshape.27), channel_id=1, replica_groups=mesh['rows'=16,'feat'=8] {'rows'}, dimensions={0} | all-to-all | bytes 262144 | tf_op jit(solution)/shard_map/all_to_all | solution.py:21
  (60 shorter events, 16.3 us)
Async XLA Ops:
  6.5 6.2 %copy-start = (s32[64,4]{0,1:T(4,128)S(1)}, s32[64,4]{0,1:T(4,128)}, u32[]{:S(2)}) copy-start(s32[64,4]{0,1:T(4,128)} %param.9) | copy-start | bytes 3076
  6.5 58.5 %all-gather.2.cloned.1.call-start = ((), (), s32[]{:S(2)}) async-start(), calls=%async_computation.1 | async-start | bytes 9437184 | tf_op jit(solution)/shard_map/all_gather | solution.py:60
Sparse Core Ops, SparseCore 0:
  12.8 52.1 all-gather.1
where the time goes:
time: 264 us; the launch traced here: 263 us
  matrix products  80.7 us (31%)
  other arithmetic  77.3 us (29%)
  waiting for transfers between devices  52.2 us (20%)
  local copies, waits for them, and re-layouts  24.1 us (9%)
  blocking collectives  14.7 us (6%)
  between operations  13.5 us (5%)
    dot_general x16, matrix products, step(): return acc + jnp.dot(onehot, block_cols, preferred_element_type=jnp.float32)  79.9 us
    eq x16, other arithmetic, step(): bin_codes[:, None, :] == bin_ids[None, :, None]  68 us
    all_gather x1, waiting for transfers between devices, shards(): grad_rows = lax.all_gather(grad_hess, 'feat', axis=0, tiled=True)  52.2 us
    dynamic_slice x16, local copies, waits for them, and re-layouts, step(): lax.dynamic_slice_in_dim(bins, block_idx * block_len, block_len, 1)  15.6 us
    all_to_all x1, blocking collectives, sum_at_owner(): blocks = lax.all_to_all(in_blocks(value, dim, size), axis, 0, 0, tiled=True)  14.7 us
    reshape x2, local copies, waits for them, and re-layouts, shards(): hist_four = hist.reshape(feat_group, BINS, 2, classes)  5.58 us
  transfers between devices with their start and end apart: 1, of which 1 were waited for; matrix products, arithmetic and copies ran while one was open for 0% of the time, Pallas kernels for 0%

commit v1 on v0

v1 whole, which is shorter than its diff:
```python
import functools

import jax
import jax.numpy as jnp
from jax import lax
from jax.experimental import pallas as pl
from jax.experimental.pallas import tpu as pltpu
from jax.sharding import PartitionSpec as P

BINS = 64
LANES = 128
GROUP = 4
BLOCK = 256
MESH = pl.DeviceIdType.MESH
bf16 = jnp.bfloat16
f8 = jnp.float8_e4m3fn
f32 = jnp.float32

l2_penalty = 1.0


def code_probs(scores):
    expon = jnp.exp(scores - jnp.max(scores, axis=0, keepdims=True))
    probs = expon * (1.0 / jnp.sum(expon, axis=0, keepdims=True))
    return jnp.where(probs > 0.5, jnp.minimum(probs - 1.0, -1e-30), probs).astype(bf16)


def grad_hess(coded, is_label):
    zero, one = jnp.zeros((), bf16), jnp.ones((), bf16)
    shift = jnp.where(coded < zero, one, zero) - jnp.where(is_label, one, zero)
    size = jnp.abs(coded)
    return coded + shift, size * (one - size)


def kernel(
    n_rows,
    n_feat,
    scores_hbm,
    labels_ref,
    bins_hbm,
    elected_ref,
    out_ref,
    scores,
    bins,
    coded,
    gh,
    acc,
    sbuf,
    rbuf,
    in_sem,
    bins_sem,
    send_sem,
    recv_sem,
    send2_sem,
    recv2_sem,
):
    n_y = n_feat // 2
    row = lax.axis_index("rows")
    feat = lax.axis_index("feat")
    y, core = feat // 2, feat % 2
    other = y * 2 + 1 - core
    plus = lax.rem(y + 1, n_y) * 2 + core
    minus = lax.rem(y + n_y - 1, n_y) * 2 + core
    sub = coded.shape[3]
    classes = coded.shape[2]
    fgrp = bins.shape[1]

    barrier = pltpu.get_barrier_semaphore()
    for peer in (other, plus, minus):
        pl.semaphore_signal(barrier, inc=1, device_id=(row, peer), device_id_type=MESH)
    for dist in range(1, n_rows):
        peer = lax.rem(row + dist, n_rows)
        pl.semaphore_signal(barrier, inc=1, device_id=(peer, feat), device_id_type=MESH)

    def source(stage, kind):
        back = jnp.where(stage == 0, 0, jnp.where(stage == 3, 2, 1))
        side = lax.rem(kind, 2)
        from_y = lax.rem(jnp.where(side == 0, y + n_y - back, y + back), n_y)
        from_core = jnp.where(kind < 2, core, 1 - core)
        half_a = jnp.where(stage == 2, 1, 0)
        half = jnp.where(side == 0, half_a, 1 - half_a)
        return from_y * 2 + from_core, half

    def bins_copy(stage, kind):
        src, half = source(stage, kind)
        start = pl.multiple_of((src * 2 + half) * sub, sub)
        slot = stage * 4 + kind
        return pltpu.make_async_copy(
            bins_hbm.at[:, pl.ds(start, sub)], bins.at[slot], bins_sem.at[slot]
        )

    copies = [
        pltpu.make_async_copy(
            scores_hbm.at[:, pl.ds(half * sub, sub)], scores.at[half], in_sem.at[half]
        )
        for half in range(2)
    ]
    for copy in copies:
        copy.start()
    for stage in range(4):
        for kind in range(4):
            bins_copy(stage, kind).start()

    for half in range(2):
        copies[half].wait()
        for lane in range(0, sub, BLOCK):
            coded[feat, half, :, lane : lane + BLOCK] = code_probs(
                scores[half, :, lane : lane + BLOCK]
            )

    pl.semaphore_wait(barrier, n_rows + 2)

    def send(src, half, peer, send_slot, recv_slot):
        return pltpu.make_async_remote_copy(
            src_ref=coded.at[src, half],
            dst_ref=coded.at[src, half],
            send_sem=send_sem.at[send_slot],
            recv_sem=recv_sem.at[recv_slot],
            device_id=(row, peer),
            device_id_type=MESH,
        )

    send(feat, 0, plus, 0, 4).start()
    send(feat, 1, minus, 1, 5).start()
    send(feat, 0, other, 2, 2).start()
    send(feat, 1, other, 3, 3).start()
    send(feat, 1, plus, 4, 8).start()
    send(feat, 0, minus, 5, 9).start()

    acc[...] = jnp.zeros_like(acc)

    class_ids = lax.broadcasted_iota(jnp.int32, (classes, LANES), 0).astype(f32).astype(bf16)

    def piece(index, carry):
        stage, kind = index // 4, lax.rem(index, 4)
        src, half = source(stage, kind)

        @pl.when((stage > 0) | (kind > 1))
        def _():
            send(src, half, other, 0, index).wait_recv()

        @pl.when((stage > 0) & (kind < 2))
        def _():
            send(src, half, other, 6 + stage * 2 + kind, index + 2).start()

        @pl.when((stage == 1) & (kind < 2))
        def _():
            onward = jnp.where(kind == 0, plus, minus)
            send(src, half, onward, 14 + kind, 12 + kind).start()

        bins_copy(stage, kind).wait()

        tiles = sub // LANES
        first = pl.multiple_of((src * 2 + half) * tiles, tiles)
        for lane in range(0, sub, LANES):
            label = labels_ref[pl.ds(first + lane // LANES, 1), :]
            label = jnp.broadcast_to(label.astype(f32), (classes, LANES)).astype(bf16)
            grad, hess = grad_hess(
                coded[src, half, :, lane : lane + LANES], label == class_ids
            )
            gh[0:classes, lane : lane + LANES] = grad
            gh[classes : 2 * classes, lane : lane + LANES] = hess

        values = gh[...]
        bin_ids = lax.broadcasted_iota(jnp.int32, (BINS, sub), 0).astype(jnp.int8)
        ones, zeros = jnp.ones((BINS, sub), f8), jnp.zeros((BINS, sub), f8)
        for group in range(fgrp // GROUP):
            onehot = []
            for feature in range(group * GROUP, (group + 1) * GROUP):
                code = bins[index, feature : feature + 1, :]
                code = jnp.broadcast_to(code, (BINS, sub)).astype(jnp.int8)
                onehot.append(jnp.where(code == bin_ids, ones, zeros))
            sums = lax.dot_general(
                values,
                jnp.concatenate(onehot, axis=0),
                (((1,), (1,)), ((), ())),
                preferred_element_type=f32,
            )
            columns = slice(group * GROUP * BINS, (group + 1) * GROUP * BINS)
            acc[:, columns] += sums
        return carry

    lax.fori_loop(0, 16, piece, 0)

    n_elect = elected_ref.shape[0]
    local = (elected_ref[...] - feat * fgrp).astype(f32)
    eye = jnp.where(
        lax.broadcasted_iota(jnp.int32, (classes, classes), 0)
        == lax.broadcasted_iota(jnp.int32, (classes, classes), 1),
        1.0,
        0.0,
    ).astype(f32)
    per_class = [
        jnp.sum(eye * local[e : e + 1, :], axis=1, keepdims=True) for e in range(n_elect)
    ]
    lane_ids = lax.broadcasted_iota(jnp.int32, (2 * classes, LANES), 1)
    upper = jnp.where(lane_ids >= BINS, 1.0, 0.0).astype(f32)
    own = classes // n_rows
    for pair in range(n_elect // 2):
        folded = []
        for e in (2 * pair, 2 * pair + 1):
            chosen = jnp.concatenate([per_class[e], per_class[e]], axis=0) - upper
            total = jnp.zeros((2 * classes, LANES), f32)
            for tile in range(fgrp // 2):
                total += jnp.where(
                    chosen == 2.0 * tile, acc[:, tile * LANES : (tile + 1) * LANES], 0.0
                )
            folded.append(total + pltpu.roll(total, BINS, 1))
        picked = jnp.where(lane_ids < BINS, folded[0], folded[1])
        columns = slice(pair * LANES, (pair + 1) * LANES)
        for owner in range(n_rows):
            sbuf[owner, 0:own, columns] = picked[owner * own : (owner + 1) * own]
            sbuf[owner, own : 2 * own, columns] = picked[
                classes + owner * own : classes + (owner + 1) * own
            ]

    def exchange(dist):
        peer = lax.rem(row + dist, n_rows)
        return pltpu.make_async_remote_copy(
            src_ref=sbuf.at[peer],
            dst_ref=rbuf.at[dist],
            send_sem=send2_sem.at[dist],
            recv_sem=recv2_sem.at[dist],
            device_id=(peer, feat),
            device_id_type=MESH,
        )

    for dist in range(1, n_rows):
        exchange(dist).start()
    total = sbuf[row]
    for dist in range(1, n_rows):
        exchange(dist).wait_recv()
        total += rbuf[dist]

    width = n_elect * BINS
    bin_of = lax.rem(lax.broadcasted_iota(jnp.int32, total.shape, 1), BINS)
    left = total
    every = total
    shift = 1
    while shift < BINS:
        left += jnp.where(bin_of >= shift, pltpu.roll(left, shift, 1), 0.0)
        every += jnp.where(
            lax.rem(bin_of, 2 * shift) < shift,
            pltpu.roll(every, width - shift, 1),
            pltpu.roll(every, shift, 1),
        )
        shift *= 2
    right = every - left
    left_g, left_h = left[:own], left[own:]
    right_g, right_h = right[:own], right[own:]
    tot_g, tot_h = every[:own], every[own:]
    gains = 0.5 * (
        left_g * left_g / (left_h + l2_penalty)
        + right_g * right_g / (right_h + l2_penalty)
        - tot_g * tot_g / (tot_h + l2_penalty)
    )
    for e in range(n_elect):
        part = gains[:, (e // 2) * LANES : (e // 2 + 1) * LANES]
        if e % 2:
            part = pltpu.roll(part, BINS, 1)
        for c in range(own):
            out_ref[c, e : e + 1, :] = part[c : c + 1, : BINS - 1]

    send(feat, 0, plus, 0, 4).wait_send()
    send(feat, 1, minus, 1, 5).wait_send()
    send(feat, 0, other, 2, 2).wait_send()
    send(feat, 1, other, 3, 3).wait_send()
    send(feat, 1, plus, 4, 8).wait_send()
    send(feat, 0, minus, 5, 9).wait_send()
    for slot in range(8, 16):
        send(feat, 0, other, slot, 0).wait_send()
    for dist in range(1, n_rows):
        exchange(dist).wait_send()


def shards(scores, labels, bins, elected):
    n_rows, n_feat = lax.axis_size("rows"), lax.axis_size("feat")
    own_rows, classes = scores.shape
    fgrp, rows = bins.shape
    n_elect = elected.shape[1]
    sub = own_rows // 2
    own = classes // n_rows
    dma = pltpu.SemaphoreType.DMA
    return pl.pallas_call(
        functools.partial(kernel, n_rows, n_feat),
        out_shape=jax.ShapeDtypeStruct((own, n_elect, BINS - 1), jnp.float32),
        in_specs=[
            pl.BlockSpec(memory_space=pl.ANY),
            pl.BlockSpec(memory_space=pltpu.VMEM),
            pl.BlockSpec(memory_space=pl.ANY),
            pl.BlockSpec(memory_space=pltpu.VMEM),
        ],
        out_specs=pl.BlockSpec(memory_space=pltpu.VMEM),
        scratch_shapes=[
            pltpu.VMEM((2, classes, sub), f32),
            pltpu.VMEM((16, fgrp, sub), jnp.int32),
            pltpu.VMEM((n_feat, 2, classes, sub), bf16),
            pltpu.VMEM((2 * classes, sub), bf16),
            pltpu.VMEM((2 * classes, fgrp * BINS), f32),
            pltpu.VMEM((n_rows, 2 * own, n_elect * BINS), f32),
            pltpu.VMEM((n_rows, 2 * own, n_elect * BINS), f32),
            dma((2,)),
            dma((16,)),
            dma((16,)),
            dma((16,)),
            dma((n_rows,)),
            dma((n_rows,)),
        ],
        compiler_params=pltpu.CompilerParams(
            collective_id=0, has_side_effects=True, vmem_limit_bytes=48 << 20
        ),
    )(scores.T, labels.reshape(rows // LANES, LANES), bins, elected.T)


def solution(mesh):
    return jax.shard_map(
        shards,
        mesh=mesh,
        in_specs=(P(("rows", "feat"), None), P("rows"), P("feat", "rows"), P(None, "feat")),
        out_specs=P("rows", "feat", None),
        check_vma=False,
    )
```

time: 264 us -> 45.4 us (0.17)
  matrix products: 80.7 us -> 0 us
  other arithmetic: 77.3 us -> 0 us
  waiting for transfers between devices: 52.2 us -> 0 us
  Pallas kernels: 0 us -> 39.6 us
  local copies, waits for them, and re-layouts: 24.1 us -> 5.6 us
  blocking collectives: 14.7 us -> 0 us
  between operations: 13.5 us -> 0.01 us
    dot_general x17 -> x0, matrix products: 80.7 us -> none  [the longest x16 79.9 us: step(): return acc + jnp.dot(onehot, block_cols, preferred_element_type=jnp.float32)]
    eq x16 -> x0, other arithmetic: 68 us -> none  [step(): bin_codes[:, None, :] == bin_ids[None, :, None]]
    all_gather x1 -> x0, waiting for transfers between devices: 52.2 us -> none  [shards(): grad_rows = lax.all_gather(grad_hess, 'feat', axis=0, tiled=True)]
    pallas_call x0 -> x1, Pallas kernels: none -> 39.6 us  [shards(): pl.pallas_call(functools.partial(kernel, n_rows, n_feat), out_shape=jax.S...]
    dynamic_slice x17 -> x0, local copies, waits for them, and re-layouts: 16.3 us -> none  [the longest x16 15.6 us: step(): lax.dynamic_slice_in_dim(bins, block_idx * block_len, block_len, 1)]
    all_to_all x1 -> x0, blocking collectives: 14.7 us -> none  [sum_at_owner(): blocks = lax.all_to_all(in_blocks(value, dim, size), axis, 0, 0, tiled=True)]
    reshape x2 -> x0, local copies, waits for them, and re-layouts: 5.58 us -> none  [shards(): hist_four = hist.reshape(feat_group, BINS, 2, classes)]
    unnamed x4 -> x9, local copies, waits for them, and re-layouts: 0.42 us -> 5.6 us
  transfers between devices with their start and end apart: 1 -> 0, of which waited for: 1 -> 0; matrix products, arithmetic and copies ran while one was open for 0% -> 0% of each run, Pallas kernels for 0% -> 0%
where the time goes in v1:
time: 45.4 us; the launch traced here: 45.2 us
  Pallas kernels  39.6 us (87%)
  local copies, waits for them, and re-layouts  5.6 us (12%)
    pallas_call x1, Pallas kernels, shards(): pl.pallas_call(functools.partial(kernel, n_rows, n_feat), out_shape=jax.S...  39.6 us
    unnamed x9, local copies, waits for them, and re-layouts  5.6 us

profile of v1, /device:TPU:0, one launch (start us, length us, event | category | flops | bytes accessed | tf_op | source)
XLA Modules:
  0.0 45.2 jit_solution(835756965940386243)
XLA Ops:
  0.0 0.0 copy-start
  0.0 2.2 %copy-done = s32[32,32768]{1,0:T(8,128)S(1)} copy-done((s32[32,32768]{1,0:T(8,128)S(1)}, s32[32,32768]{1,0:T(8,128)}, u32[]{:S(2)}) %copy-start) | copy-done | bytes 4194328
  2.2 0.0 copy-start.1
  2.2 1.2 %copy-done.1 = f32[4096,64]{0,1:T(8,128)S(1)} copy-done((f32[4096,64]{0,1:T(8,128)S(1)}, f32[4096,64]{0,1:T(8,128)}, u32[]{:S(2)}) %copy-start.1) | copy-done | bytes 1048600
  3.4 0.0 copy-start.2
  3.4 0.9 %copy-done.2 = s32[32768]{0:T(1024)S(1)} copy-done((s32[32768]{0:T(1024)S(1)}, s32[32768]{0:T(1024)}, u32[]{:S(2)}) %copy-start.2) | copy-done | bytes 131096
  4.3 0.0 copy-start.3
  4.3 0.7 %copy-done.3 = s32[64,4]{0,1:T(4,128)S(1)} copy-done((s32[64,4]{0,1:T(4,128)S(1)}, s32[64,4]{0,1:T(4,128)}, u32[]{:S(2)}) %copy-start.3) | copy-done | bytes 1048
  5.0 39.6 %shard_map.46 = f32[4,4,63]{2,1,0:T(4,128)S(1)} custom-call(f32[64,4096]{1,0:T(8,128)S(1)} %bitcast.3, s32[256,128]{1,0:T(8,128)S(1)} %bitcast.4, s32[32,32768]{1,0:T(8,128)S(1)} %copy-done, s32[4,64]{1,0:T(4,128)S(1)} %bitcast.5), custom_call_target="tpu_custom_call" | custom-call | tf_op jit(solution)/shard_map/pallas_call | solution.py:284
  44.6 0.6 %copy.6 = f32[4,4,63]{2,1,0:T(4,128)} copy(f32[4,4,63]{2,1,0:T(4,128)S(1)} %shard_map.46) | data formatting | bytes 8064
Async XLA Ops:
  0.0 2.2 %copy-start = (s32[32,32768]{1,0:T(8,128)S(1)}, s32[32,32768]{1,0:T(8,128)}, u32[]{:S(2)}) copy-start(s32[32,32768]{1,0:T(8,128)} %bins_hbm.1) | copy-start | bytes 12582916
  2.2 1.2 %copy-start.1 = (f32[4096,64]{0,1:T(8,128)S(1)}, f32[4096,64]{0,1:T(8,128)}, u32[]{:S(2)}) copy-start(f32[4096,64]{0,1:T(8,128)} %param.4) | copy-start | bytes 3145732
  3.4 0.9 %copy-start.2 = (s32[32768]{0:T(1024)S(1)}, s32[32768]{0:T(1024)}, u32[]{:S(2)}) copy-start(s32[32768]{0:T(1024)} %param.5) | copy-start | bytes 393220
  4.3 0.7 %copy-start.3 = (s32[64,4]{0,1:T(4,128)S(1)}, s32[64,4]{0,1:T(4,128)}, u32[]{:S(2)}) copy-start(s32[64,4]{0,1:T(4,128)} %param.7) | copy-start | bytes 3076

commit v2 on v1

v2 whole, which is shorter than its diff:
```python
import functools
import math

import jax
import jax.numpy as jnp
from jax import lax
from jax.experimental import pallas as pl
from jax.experimental.pallas import tpu as pltpu
from jax.sharding import PartitionSpec as P

BINS = 64
LANES = 128
GROUP = 4
PIECES = 32
UNITS = PIECES // 2
X_CHIPS = 4
BLOCK = 256
MESH = pl.DeviceIdType.MESH
bf16 = jnp.bfloat16
f8 = jnp.float8_e4m3fn
f32 = jnp.float32

l2_penalty = 1.0


def code_probs(scores):
    expon = jnp.exp(scores - jnp.max(scores, axis=0, keepdims=True))
    probs = expon * (1.0 / jnp.sum(expon, axis=0, keepdims=True))
    return jnp.where(probs > 0.5, jnp.minimum(probs - 1.0, -1e-30), probs).astype(bf16)


def grad_hess(coded, is_label):
    zero, one = jnp.zeros((), bf16), jnp.ones((), bf16)
    shift = jnp.where(coded < zero, one, zero) - jnp.where(is_label, one, zero)
    size = jnp.abs(coded)
    return coded + shift, size * (one - size)


def kernel(
    n_rows,
    n_x,
    n_feat,
    scores_hbm,
    labels_hbm,
    bins_hbm,
    elected_hbm,
    out_ref,
    scores,
    labels,
    bins,
    elected,
    coded,
    gh,
    acc,
    sbuf,
    rbuf,
    in_sem,
    bins_sem,
    send_sem,
    recv_sem,
    send2_sem,
    recv2_sem,
    all_in,
):
    n_y, n_z = n_feat // 2, n_rows // n_x
    row = lax.axis_index("rows")
    feat = lax.axis_index("feat")
    y, core = feat // 2, feat % 2
    z, x = row // n_x, row % n_x
    other = y * 2 + 1 - core
    plus = lax.rem(y + 1, n_y) * 2 + core
    minus = lax.rem(y + n_y - 1, n_y) * 2 + core
    sub = coded.shape[3]
    classes = coded.shape[2]
    fgrp = bins.shape[1]

    barrier = pltpu.get_barrier_semaphore()
    for peer in (other, plus, minus):
        pl.semaphore_signal(barrier, inc=1, device_id=(row, peer), device_id_type=MESH)
    for dist in range(1, n_x):
        peer = z * n_x + lax.rem(x + dist, n_x)
        pl.semaphore_signal(barrier, inc=1, device_id=(peer, feat), device_id_type=MESH)
    for dist in range(1, n_z):
        peer = lax.rem(z + dist, n_z) * n_x + x
        pl.semaphore_signal(barrier, inc=1, device_id=(peer, feat), device_id_type=MESH)

    def source(index):
        stage, kind = index // 4, lax.rem(index, 4)
        back = jnp.where(stage < 6, 1, 2)
        side = lax.rem(kind, 2)
        from_y = lax.rem(jnp.where(side == 0, y + n_y - back, y + back), n_y)
        from_core = jnp.where(kind < 2, core, 1 - core)
        near = jnp.where(stage == 0, feat, other)
        src = jnp.where(stage < 2, near, from_y * 2 + from_core)
        nth = jnp.where(stage < 2, kind // 2, jnp.where(stage < 6, stage - 2, stage - 6))
        return src, jnp.where(side == 0, nth, 3 - nth)

    def bins_copy(unit, side):
        src, quarter = source(2 * unit + side)
        start = pl.multiple_of((src * 4 + quarter) * sub, sub)
        return pltpu.make_async_copy(
            bins_hbm.at[:, pl.ds(start, sub)],
            bins.at[unit, :, pl.ds(side * sub, sub)],
            bins_sem.at[2 * unit + side],
        )

    own_order = (0, 3, 1, 2)
    copies = [
        pltpu.make_async_copy(
            scores_hbm.at[:, pl.ds(quarter * sub, sub)], scores.at[quarter], in_sem.at[quarter]
        )
        for quarter in own_order
    ]
    small = [
        pltpu.make_async_copy(labels_hbm, labels, in_sem.at[4]),
        pltpu.make_async_copy(elected_hbm, elected, in_sem.at[5]),
    ]
    for copy in copies + small:
        copy.start()

    def start_bins(unit, carry):
        bins_copy(unit, 0).start()
        bins_copy(unit, 1).start()
        return carry

    lax.fori_loop(0, UNITS, start_bins, 0)

    for quarter, copy in zip(own_order, copies):
        copy.wait()
        for lane in range(0, sub, BLOCK):
            lanes = slice(lane, min(lane + BLOCK, sub))
            coded[feat, quarter, :, lanes] = code_probs(scores[quarter, :, lanes])

    def send(src, quarter, peer, send_slot, recv_slot):
        return pltpu.make_async_remote_copy(
            src_ref=coded.at[src, quarter],
            dst_ref=coded.at[src, quarter],
            send_sem=send_sem.at[send_slot],
            recv_sem=recv_sem.at[recv_slot],
            device_id=(row, peer),
            device_id_type=MESH,
        )

    own_sends = []
    for nth in range(4):
        own_sends.append(send(feat, nth, plus, nth, 8 + 4 * nth))
        own_sends.append(send(feat, 3 - nth, minus, 4 + nth, 9 + 4 * nth))
        own_sends.append(send(feat, own_order[nth], other, 8 + nth, 4 + nth))

    acc[...] = jnp.zeros_like(acc)

    class_ids = lax.broadcasted_iota(jnp.int32, (classes, LANES), 0).astype(f32).astype(bf16)

    def receive(unit):
        stage, kind = unit // 2, 2 * lax.rem(unit, 2)
        pieces = [source(2 * unit + side) for side in range(2)]
        for side in range(2):
            send(*pieces[side], other, 0, 2 * unit + side).wait_recv()

        @pl.when((stage > 1) & (kind == 0))
        def _():
            for side in range(2):
                slot = 8 + stage * 2 + side
                send(*pieces[side], other, slot, 2 * unit + side + 2).start()

        @pl.when(((stage == 2) | (stage == 3)) & (kind == 0))
        def _():
            for side, onward in enumerate((plus, minus)):
                slot = 20 + stage * 2 + side
                send(*pieces[side], onward, slot, 2 * unit + side + 16).start()

        for side in range(2):
            bins_copy(unit, side).wait()

    tiles = sub // LANES
    groups = fgrp // GROUP

    def decode(unit):
        for tile in range(2 * tiles):
            src, quarter = source(2 * unit + tile // tiles)
            first = pl.multiple_of((src * 4 + quarter) * tiles, tiles)
            label = labels[pl.ds(first + tile % tiles, 1), :].astype(f32)
            label = jnp.broadcast_to(label, (classes, LANES)).astype(bf16)
            column = tile % tiles * LANES
            grad, hess = grad_hess(
                coded[src, quarter, :, column : column + LANES], label == class_ids
            )
            lanes = slice(tile * LANES, (tile + 1) * LANES)
            gh[0:classes, lanes] = grad
            gh[classes : 2 * classes, lanes] = hess

    def add_unit(unit):
        decode(unit)
        values = gh[...]
        shape = (BINS, 2 * sub)
        bin_ids = lax.broadcasted_iota(jnp.int32, shape, 0).astype(jnp.int8)
        ones, zeros = jnp.ones(shape, f8), jnp.zeros(shape, f8)
        for group in range(groups):
            onehot = []
            for feature in range(group * GROUP, (group + 1) * GROUP):
                code = bins[unit, feature : feature + 1, :]
                code = jnp.broadcast_to(code, shape).astype(jnp.int8)
                onehot.append(jnp.where(code == bin_ids, ones, zeros))
            columns = slice(group * GROUP * BINS, (group + 1) * GROUP * BINS)
            acc[:, columns] += lax.dot_general(
                values,
                jnp.concatenate(onehot, axis=0),
                (((1,), (1,)), ((), ())),
                preferred_element_type=f32,
            )

    for copy in small:
        copy.wait()

    def own_unit(unit):
        bins_copy(unit, 0).wait()
        bins_copy(unit, 1).wait()
        add_unit(unit)

    own_unit(0)
    pl.semaphore_wait(barrier, n_x + n_z + 1)
    for copy in own_sends:
        copy.start()
    for dist in range(1, n_x):
        peer = z * n_x + lax.rem(x + dist, n_x)
        pl.semaphore_signal(all_in, inc=1, device_id=(peer, feat), device_id_type=MESH)
    own_unit(1)

    def next_unit(unit, carry):
        receive(unit)
        add_unit(unit)
        return carry

    lax.fori_loop(2, UNITS, next_unit, 0)

    n_elect = elected.shape[0]
    local = (elected[...] - feat * fgrp).astype(f32)
    eye = jnp.where(
        lax.broadcasted_iota(jnp.int32, (classes, classes), 0)
        == lax.broadcasted_iota(jnp.int32, (classes, classes), 1),
        1.0,
        0.0,
    ).astype(f32)
    per_class = [
        jnp.sum(eye * local[e : e + 1, :], axis=1, keepdims=True) for e in range(n_elect)
    ]
    lane_ids = lax.broadcasted_iota(jnp.int32, (2 * classes, LANES), 1)
    upper = jnp.where(lane_ids >= BINS, 1.0, 0.0).astype(f32)
    own = classes // n_rows
    for pair in range(n_elect // 2):
        folded = []
        for e in (2 * pair, 2 * pair + 1):
            chosen = jnp.concatenate([per_class[e], per_class[e]], axis=0) - upper
            total = jnp.zeros((2 * classes, LANES), f32)
            for tile in range(fgrp // 2):
                total += jnp.where(
                    chosen == 2.0 * tile, acc[:, tile * LANES : (tile + 1) * LANES], 0.0
                )
            folded.append(total + pltpu.roll(total, BINS, 1))
        picked = jnp.where(lane_ids < BINS, folded[0], folded[1])
        columns = slice(pair * LANES, (pair + 1) * LANES)
        for owner in range(n_rows):
            sbuf[owner, 0:own, columns] = picked[owner * own : (owner + 1) * own]
            sbuf[owner, own : 2 * own, columns] = picked[
                classes + owner * own : classes + (owner + 1) * own
            ]

    def exchange(dist):
        peer = lax.rem(row + dist, n_rows)
        return pltpu.make_async_remote_copy(
            src_ref=sbuf.at[peer],
            dst_ref=rbuf.at[dist],
            send_sem=send2_sem.at[dist],
            recv_sem=recv2_sem.at[dist],
            device_id=(peer, feat),
            device_id_type=MESH,
        )

    pl.semaphore_wait(all_in, n_x - 1)
    for dist in range(1, n_rows):
        exchange(dist).start()
    total = sbuf[row]
    for dist in range(1, n_rows):
        exchange(dist).wait_recv()
        total += rbuf[dist]

    width = n_elect * BINS
    bin_of = lax.rem(lax.broadcasted_iota(jnp.int32, total.shape, 1), BINS)
    left = total
    every = total
    shift = 1
    while shift < BINS:
        left += jnp.where(bin_of >= shift, pltpu.roll(left, shift, 1), 0.0)
        every += jnp.where(
            lax.rem(bin_of, 2 * shift) < shift,
            pltpu.roll(every, width - shift, 1),
            pltpu.roll(every, shift, 1),
        )
        shift *= 2
    right = every - left
    left_g, left_h = left[:own], left[own:]
    right_g, right_h = right[:own], right[own:]
    tot_g, tot_h = every[:own], every[own:]
    gains = 0.5 * (
        left_g * left_g / (left_h + l2_penalty)
        + right_g * right_g / (right_h + l2_penalty)
        - tot_g * tot_g / (tot_h + l2_penalty)
    )
    for e in range(n_elect):
        part = gains[:, (e // 2) * LANES : (e // 2 + 1) * LANES]
        if e % 2:
            part = pltpu.roll(part, BINS, 1)
        for c in range(own):
            out_ref[c, e : e + 1, :] = part[c : c + 1, : BINS - 1]

    for copy in own_sends:
        copy.wait_send()
    for slot in range(12, 28):
        send(feat, 0, other, slot, 0).wait_send()
    for dist in range(1, n_rows):
        exchange(dist).wait_send()


def shards(scores, labels, bins, elected):
    n_rows, n_feat = lax.axis_size("rows"), lax.axis_size("feat")
    own_rows, classes = scores.shape
    fgrp, rows = bins.shape
    n_elect = elected.shape[1]
    sub = own_rows // 4
    own = classes // n_rows
    n_x = math.gcd(n_rows, X_CHIPS)
    dma = pltpu.SemaphoreType.DMA
    return pl.pallas_call(
        functools.partial(kernel, n_rows, n_x, n_feat),
        out_shape=jax.ShapeDtypeStruct((own, n_elect, BINS - 1), jnp.float32),
        in_specs=[pl.BlockSpec(memory_space=pl.ANY)] * 4,
        out_specs=pl.BlockSpec(memory_space=pltpu.VMEM),
        scratch_shapes=[
            pltpu.VMEM((4, classes, sub), f32),
            pltpu.VMEM((rows // LANES, LANES), jnp.int32),
            pltpu.VMEM((UNITS, fgrp, 2 * sub), jnp.int32),
            pltpu.VMEM((n_elect, classes), jnp.int32),
            pltpu.VMEM((n_feat, 4, classes, sub), bf16),
            pltpu.VMEM((2 * classes, 2 * sub), bf16),
            pltpu.VMEM((2 * classes, fgrp * BINS), f32),
            pltpu.VMEM((n_rows, 2 * own, n_elect * BINS), f32),
            pltpu.VMEM((n_rows, 2 * own, n_elect * BINS), f32),
            dma((6,)),
            dma((PIECES,)),
            dma((28,)),
            dma((PIECES,)),
            dma((n_rows,)),
            dma((n_rows,)),
            pltpu.SemaphoreType.REGULAR,
        ],
        compiler_params=pltpu.CompilerParams(
            collective_id=0, has_side_effects=True, vmem_limit_bytes=60 << 20
        ),
    )(scores.T, labels.reshape(rows // LANES, LANES), bins, elected.T)


def solution(mesh):
    return jax.shard_map(
        shards,
        mesh=mesh,
        in_specs=(P(("rows", "feat"), None), P("rows"), P("feat", "rows"), P(None, "feat")),
        out_specs=P("rows", "feat", None),
        check_vma=False,
    )
```

time: 45.4 us -> 40.5 us (0.89)
  local copies, waits for them, and re-layouts: 5.6 us -> 1.3 us
  Pallas kernels: 39.6 us -> 39 us
    unnamed x9 -> x1, local copies, waits for them, and re-layouts: 5.6 us -> 1.3 us
    pallas_call x1, Pallas kernels: 39.6 us -> 39 us  [shards(): pl.pallas_call(functools.partial(kernel, n_rows, n_x, n_feat), out_shape=...]
where the time goes in v2:
time: 40.5 us; the launch traced here: 40.3 us
  Pallas kernels  39 us (96%)
  local copies, waits for them, and re-layouts  1.3 us (3%)
    pallas_call x1, Pallas kernels, shards(): pl.pallas_call(functools.partial(kernel, n_rows, n_x, n_feat), out_shape=...  39 us
    unnamed x1, local copies, waits for them, and re-layouts  1.3 us

profile of v2, /device:TPU:0, one launch (start us, length us, event | category | flops | bytes accessed | tf_op | source)
XLA Modules:
  0.0 40.3 jit_solution(2516414802729628599)
XLA Ops:
  0.0 39.0 %shard_map.46 = f32[4,4,63]{2,1,0:T(4,128)} custom-call(f32[64,4096]{1,0:T(8,128)} %bitcast.3, s32[256,128]{1,0:T(8,128)} %bitcast.4, s32[32,32768]{1,0:T(8,128)} %bins_hbm.1, s32[4,64]{1,0:T(4,128)} %bitcast.5), custom_call_target="tpu_custom_call" | custom-call | tf_op jit(solution)/shard_map/pallas_call | solution.py:333
  39.0 1.3 %copy.6 = f32[4,4,63]{2,1,0:T(4,128)} copy(f32[4,4,63]{2,1,0:T(4,128)} %shard_map.46) | data formatting | bytes 8064

commit v3 on v2

--- a/solution.py
+++ b/solution.py
@@ -52,6 +52,8 @@
     coded,
     gh,
     acc,
+    chosen,
+    picked,
     sbuf,
     rbuf,
     in_sem,
@@ -189,7 +191,15 @@
             gh[0:classes, lanes] = grad
             gh[classes : 2 * classes, lanes] = hess
 
-    def add_unit(unit):
+    def select(group):
+        for e in range(elected.shape[0]):
+            total = picked[e]
+            for tile in range(group * GROUP // 2, (group + 1) * GROUP // 2):
+                lanes = slice(tile * LANES, (tile + 1) * LANES)
+                total += jnp.where(chosen[e] == 2.0 * tile, acc[:, lanes], 0.0)
+            picked[e] = total
+
+    def add_unit(unit, last=False):
         decode(unit)
         values = gh[...]
         shape = (BINS, 2 * sub)
@@ -208,6 +218,10 @@
                 (((1,), (1,)), ((), ())),
                 preferred_element_type=f32,
             )
+            if last and group > 0:
+                select(group - 1)
+        if last:
+            select(groups - 1)
 
     for copy in small:
         copy.wait()
@@ -216,22 +230,6 @@
         bins_copy(unit, 0).wait()
         bins_copy(unit, 1).wait()
         add_unit(unit)
-
-    own_unit(0)
-    pl.semaphore_wait(barrier, n_x + n_z + 1)
-    for copy in own_sends:
-        copy.start()
-    for dist in range(1, n_x):
-        peer = z * n_x + lax.rem(x + dist, n_x)
-        pl.semaphore_signal(all_in, inc=1, device_id=(peer, feat), device_id_type=MESH)
-    own_unit(1)
-
-    def next_unit(unit, carry):
-        receive(unit)
-        add_unit(unit)
-        return carry
-
-    lax.fori_loop(2, UNITS, next_unit, 0)
 
     n_elect = elected.shape[0]
     local = (elected[...] - feat * fgrp).astype(f32)
@@ -241,48 +239,67 @@
         1.0,
         0.0,
     ).astype(f32)
-    per_class = [
-        jnp.sum(eye * local[e : e + 1, :], axis=1, keepdims=True) for e in range(n_elect)
-    ]
     lane_ids = lax.broadcasted_iota(jnp.int32, (2 * classes, LANES), 1)
     upper = jnp.where(lane_ids >= BINS, 1.0, 0.0).astype(f32)
+    for e in range(n_elect):
+        per_class = jnp.sum(eye * local[e : e + 1, :], axis=1, keepdims=True)
+        chosen[e] = jnp.concatenate([per_class, per_class], axis=0) - upper
+        picked[e] = jnp.zeros((2 * classes, LANES), f32)
     own = classes // n_rows
+
+    pl.semaphore_wait(barrier, n_x + n_z + 1)
+    for copy in own_sends:
+        copy.start()
+    for dist in range(1, n_x):
+        peer = z * n_x + lax.rem(x + dist, n_x)
+        pl.semaphore_signal(all_in, inc=1, device_id=(peer, feat), device_id_type=MESH)
+    own_unit(0)
+    own_unit(1)
+
+    def next_unit(unit, carry):
+        receive(unit)
+        add_unit(unit)
+        return carry
+
+    lax.fori_loop(2, UNITS - 1, next_unit, 0)
+    receive(UNITS - 1)
+    add_unit(UNITS - 1, last=True)
+
+    def exchange(pair, dist_z, dist_x):
+        to_z, to_x = lax.rem(z + dist_z, n_z), lax.rem(x + dist_x, n_x)
+        peer = to_z * n_x + to_x
+        slot = dist_z * n_x + dist_x
+        return pltpu.make_async_remote_copy(
+            src_ref=sbuf.at[pair, peer],
+            dst_ref=rbuf.at[pair, slot],
+            send_sem=send2_sem.at[pair * n_rows + slot],
+            recv_sem=recv2_sem.at[pair * n_rows + slot],
+            device_id=(peer, feat),
+            device_id_type=MESH,
+        )
+
+    dists = [(dist_z, dist_x) for dist_z in range(n_z) for dist_x in range(n_x)][1:]
+    dists.sort(key=lambda d: -min(d[0], n_z - d[0]) - min(d[1], n_x - d[1]))
+
+    pl.semaphore_wait(all_in, n_x - 1)
     for pair in range(n_elect // 2):
-        folded = []
-        for e in (2 * pair, 2 * pair + 1):
-            chosen = jnp.concatenate([per_class[e], per_class[e]], axis=0) - upper
-            total = jnp.zeros((2 * classes, LANES), f32)
-            for tile in range(fgrp // 2):
-                total += jnp.where(
-                    chosen == 2.0 * tile, acc[:, tile * LANES : (tile + 1) * LANES], 0.0
-                )
-            folded.append(total + pltpu.roll(total, BINS, 1))
-        picked = jnp.where(lane_ids < BINS, folded[0], folded[1])
-        columns = slice(pair * LANES, (pair + 1) * LANES)
+        folded = [picked[e] + pltpu.roll(picked[e], BINS, 1) for e in (2 * pair, 2 * pair + 1)]
+        both = jnp.where(lane_ids < BINS, folded[0], folded[1])
         for owner in range(n_rows):
-            sbuf[owner, 0:own, columns] = picked[owner * own : (owner + 1) * own]
-            sbuf[owner, own : 2 * own, columns] = picked[
+            sbuf[pair, owner, 0:own] = both[owner * own : (owner + 1) * own]
+            sbuf[pair, owner, own : 2 * own] = both[
                 classes + owner * own : classes + (owner + 1) * own
             ]
-
-    def exchange(dist):
-        peer = lax.rem(row + dist, n_rows)
-        return pltpu.make_async_remote_copy(
-            src_ref=sbuf.at[peer],
-            dst_ref=rbuf.at[dist],
-            send_sem=send2_sem.at[dist],
-            recv_sem=recv2_sem.at[dist],
-            device_id=(peer, feat),
-            device_id_type=MESH,
-        )
-
-    pl.semaphore_wait(all_in, n_x - 1)
-    for dist in range(1, n_rows):
-        exchange(dist).start()
-    total = sbuf[row]
-    for dist in range(1, n_rows):
-        exchange(dist).wait_recv()
-        total += rbuf[dist]
+        for dist in dists:
+            exchange(pair, *dist).start()
+    totals = []
+    for pair in range(n_elect // 2):
+        total = sbuf[pair, row]
+        for dist in reversed(dists):
+            exchange(pair, *dist).wait_recv()
+            total += rbuf[pair, dist[0] * n_x + dist[1]]
+        totals.append(total)
+    total = jnp.concatenate(totals, axis=1)
 
     width = n_elect * BINS
     bin_of = lax.rem(lax.broadcasted_iota(jnp.int32, total.shape, 1), BINS)
@@ -317,8 +334,9 @@
         copy.wait_send()
     for slot in range(12, 28):
         send(feat, 0, other, slot, 0).wait_send()
-    for dist in range(1, n_rows):
-        exchange(dist).wait_send()
+    for pair in range(n_elect // 2):
+        for dist in dists:
+            exchange(pair, *dist).wait_send()
 
 
 def shards(scores, labels, bins, elected):
@@ -332,7 +350,7 @@
     dma = pltpu.SemaphoreType.DMA
     return pl.pallas_call(
         functools.partial(kernel, n_rows, n_x, n_feat),
-        out_shape=jax.ShapeDtypeStruct((own, n_elect, BINS - 1), jnp.float32),
+        out_shape=pltpu.VMEM((own, n_elect, BINS - 1), jnp.float32),
         in_specs=[pl.BlockSpec(memory_space=pl.ANY)] * 4,
         out_specs=pl.BlockSpec(memory_space=pltpu.VMEM),
         scratch_shapes=[
@@ -343,14 +361,16 @@
             pltpu.VMEM((n_feat, 4, classes, sub), bf16),
             pltpu.VMEM((2 * classes, 2 * sub), bf16),
             pltpu.VMEM((2 * classes, fgrp * BINS), f32),
-            pltpu.VMEM((n_rows, 2 * own, n_elect * BINS), f32),
-            pltpu.VMEM((n_rows, 2 * own, n_elect * BINS), f32),
+            pltpu.VMEM((n_elect, 2 * classes, LANES), f32),
+            pltpu.VMEM((n_elect, 2 * classes, LANES), f32),
+            pltpu.VMEM((n_elect // 2, n_rows, 2 * own, LANES), f32),
+            pltpu.VMEM((n_elect // 2, n_rows, 2 * own, LANES), f32),
             dma((6,)),
             dma((PIECES,)),
             dma((28,)),
             dma((PIECES,)),
-            dma((n_rows,)),
-            dma((n_rows,)),
+            dma((n_elect // 2 * n_rows,)),
+            dma((n_elect // 2 * n_rows,)),
             pltpu.SemaphoreType.REGULAR,
         ],
         compiler_params=pltpu.CompilerParams(

time: 40.5 us -> 38.8 us (0.958)
  Pallas kernels: 39 us -> 37.8 us
  local copies, waits for them, and re-layouts: 1.3 us -> 0.6 us
    pallas_call x1, Pallas kernels: 39 us -> 37.8 us  [shards(): pl.pallas_call(functools.partial(kernel, n_rows, n_x, n_feat), out_shape=...]
    unnamed x1, local copies, waits for them, and re-layouts: 1.3 us -> 0.6 us
where the time goes in v3:
time: 38.8 us; the launch traced here: 38.4 us
  Pallas kernels  37.8 us (97%)
  local copies, waits for them, and re-layouts  0.6 us (2%)
    pallas_call x1, Pallas kernels, shards(): pl.pallas_call(functools.partial(kernel, n_rows, n_x, n_feat), out_shape=...  37.8 us

profile of v3, /device:TPU:0, one launch (start us, length us, event | category | flops | bytes accessed | tf_op | source)
XLA Modules:
  0.0 38.4 jit_solution(17654332065950993123)
XLA Ops:
  0.0 37.8 %shard_map.46 = f32[4,4,63]{2,1,0:T(4,128)S(1)} custom-call(f32[64,4096]{1,0:T(8,128)} %bitcast.3, s32[256,128]{1,0:T(8,128)} %bitcast.4, s32[32,32768]{1,0:T(8,128)} %bins_hbm.1, s32[4,64]{1,0:T(4,128)} %bitcast.5), custom_call_target="tpu_custom_call" | custom-call | tf_op jit(solution)/shard_map/pallas_call | solution.py:351
  37.8 0.6 %copy.6 = f32[4,4,63]{2,1,0:T(4,128)} copy(f32[4,4,63]{2,1,0:T(4,128)S(1)} %shard_map.46) | data formatting | bytes 8064

commit v4 on v3

--- a/solution.py
+++ b/solution.py
@@ -57,7 +57,6 @@
     sbuf,
     rbuf,
     in_sem,
-    bins_sem,
     send_sem,
     recv_sem,
     send2_sem,
@@ -74,7 +73,7 @@
     minus = lax.rem(y + n_y - 1, n_y) * 2 + core
     sub = coded.shape[3]
     classes = coded.shape[2]
-    fgrp = bins.shape[1]
+    fgrp = bins.shape[0]
 
     barrier = pltpu.get_barrier_semaphore()
     for peer in (other, plus, minus):
@@ -97,15 +96,6 @@
         nth = jnp.where(stage < 2, kind // 2, jnp.where(stage < 6, stage - 2, stage - 6))
         return src, jnp.where(side == 0, nth, 3 - nth)
 
-    def bins_copy(unit, side):
-        src, quarter = source(2 * unit + side)
-        start = pl.multiple_of((src * 4 + quarter) * sub, sub)
-        return pltpu.make_async_copy(
-            bins_hbm.at[:, pl.ds(start, sub)],
-            bins.at[unit, :, pl.ds(side * sub, sub)],
-            bins_sem.at[2 * unit + side],
-        )
-
     own_order = (0, 3, 1, 2)
     copies = [
         pltpu.make_async_copy(
@@ -116,19 +106,14 @@
     small = [
         pltpu.make_async_copy(labels_hbm, labels, in_sem.at[4]),
         pltpu.make_async_copy(elected_hbm, elected, in_sem.at[5]),
+        pltpu.make_async_copy(bins_hbm, bins, in_sem.at[6]),
     ]
     for copy in copies + small:
         copy.start()
 
-    def start_bins(unit, carry):
-        bins_copy(unit, 0).start()
-        bins_copy(unit, 1).start()
-        return carry
-
-    lax.fori_loop(0, UNITS, start_bins, 0)
-
-    for quarter, copy in zip(own_order, copies):
-        copy.wait()
+    def code_own(nth):
+        quarter = own_order[nth]
+        copies[nth].wait()
         for lane in range(0, sub, BLOCK):
             lanes = slice(lane, min(lane + BLOCK, sub))
             coded[feat, quarter, :, lanes] = code_probs(scores[quarter, :, lanes])
@@ -143,12 +128,29 @@
             device_id_type=MESH,
         )
 
-    own_sends = []
-    for nth in range(4):
-        own_sends.append(send(feat, nth, plus, nth, 8 + 4 * nth))
-        own_sends.append(send(feat, 3 - nth, minus, 4 + nth, 9 + 4 * nth))
-        own_sends.append(send(feat, own_order[nth], other, 8 + nth, 4 + nth))
-
+    own_sends = [
+        (
+            send(feat, nth, plus, nth, 8 + 4 * nth),
+            send(feat, 3 - nth, minus, 4 + nth, 9 + 4 * nth),
+            send(feat, own_order[nth], other, 8 + nth, 4 + nth),
+        )
+        for nth in range(4)
+    ]
+    to_plus, to_minus, to_other = zip(*own_sends)
+    code_own(0)
+    code_own(1)
+    pl.semaphore_wait(barrier, n_x + n_z + 1)
+    for copy in (to_plus[0], to_minus[0], *to_other[:2]):
+        copy.start()
+    code_own(2)
+    code_own(3)
+    for copy in (to_plus[1], to_minus[1], to_plus[2], to_minus[2], to_plus[3], to_minus[3]):
+        copy.start()
+    for copy in to_other[2:]:
+        copy.start()
+    for dist in range(1, n_x):
+        peer = z * n_x + lax.rem(x + dist, n_x)
+        pl.semaphore_signal(all_in, inc=1, device_id=(peer, feat), device_id_type=MESH)
     acc[...] = jnp.zeros_like(acc)
 
     class_ids = lax.broadcasted_iota(jnp.int32, (classes, LANES), 0).astype(f32).astype(bf16)
@@ -170,9 +172,6 @@
             for side, onward in enumerate((plus, minus)):
                 slot = 20 + stage * 2 + side
                 send(*pieces[side], onward, slot, 2 * unit + side + 16).start()
-
-        for side in range(2):
-            bins_copy(unit, side).wait()
 
     tiles = sub // LANES
     groups = fgrp // GROUP
@@ -202,13 +201,17 @@
     def add_unit(unit, last=False):
         decode(unit)
         values = gh[...]
+        pieces = [source(2 * unit + side) for side in range(2)]
+        starts = [pl.multiple_of((src * 4 + quarter) * sub, sub) for src, quarter in pieces]
         shape = (BINS, 2 * sub)
         bin_ids = lax.broadcasted_iota(jnp.int32, shape, 0).astype(jnp.int8)
         ones, zeros = jnp.ones(shape, f8), jnp.zeros(shape, f8)
         for group in range(groups):
             onehot = []
             for feature in range(group * GROUP, (group + 1) * GROUP):
-                code = bins[unit, feature : feature + 1, :]
+                code = jnp.concatenate(
+                    [bins[feature : feature + 1, pl.ds(start, sub)] for start in starts], axis=1
+                )
                 code = jnp.broadcast_to(code, shape).astype(jnp.int8)
                 onehot.append(jnp.where(code == bin_ids, ones, zeros))
             columns = slice(group * GROUP * BINS, (group + 1) * GROUP * BINS)
@@ -225,11 +228,6 @@
 
     for copy in small:
         copy.wait()
-
-    def own_unit(unit):
-        bins_copy(unit, 0).wait()
-        bins_copy(unit, 1).wait()
-        add_unit(unit)
 
     n_elect = elected.shape[0]
     local = (elected[...] - feat * fgrp).astype(f32)
@@ -247,14 +245,8 @@
         picked[e] = jnp.zeros((2 * classes, LANES), f32)
     own = classes // n_rows
 
-    pl.semaphore_wait(barrier, n_x + n_z + 1)
-    for copy in own_sends:
-        copy.start()
-    for dist in range(1, n_x):
-        peer = z * n_x + lax.rem(x + dist, n_x)
-        pl.semaphore_signal(all_in, inc=1, device_id=(peer, feat), device_id_type=MESH)
-    own_unit(0)
-    own_unit(1)
+    add_unit(0)
+    add_unit(1)
 
     def next_unit(unit, carry):
         receive(unit)
@@ -330,7 +322,7 @@
         for c in range(own):
             out_ref[c, e : e + 1, :] = part[c : c + 1, : BINS - 1]
 
-    for copy in own_sends:
+    for copy in to_plus + to_minus + to_other:
         copy.wait_send()
     for slot in range(12, 28):
         send(feat, 0, other, slot, 0).wait_send()
@@ -356,7 +348,7 @@
         scratch_shapes=[
             pltpu.VMEM((4, classes, sub), f32),
             pltpu.VMEM((rows // LANES, LANES), jnp.int32),
-            pltpu.VMEM((UNITS, fgrp, 2 * sub), jnp.int32),
+            pltpu.VMEM((fgrp, rows), jnp.int32),
             pltpu.VMEM((n_elect, classes), jnp.int32),
             pltpu.VMEM((n_feat, 4, classes, sub), bf16),
             pltpu.VMEM((2 * classes, 2 * sub), bf16),
@@ -365,8 +357,7 @@
             pltpu.VMEM((n_elect, 2 * classes, LANES), f32),
             pltpu.VMEM((n_elect // 2, n_rows, 2 * own, LANES), f32),
             pltpu.VMEM((n_elect // 2, n_rows, 2 * own, LANES), f32),
-            dma((6,)),
-            dma((PIECES,)),
+            dma((7,)),
             dma((28,)),
             dma((PIECES,)),
             dma((n_elect // 2 * n_rows,)),

time: 38.8 us -> 38.8 us (level)
  no operation moved by 1% of the time
where the time goes in v4:
time: 38.8 us; the launch traced here: 38.4 us
  Pallas kernels  37.8 us (97%)
  local copies, waits for them, and re-layouts  0.6 us (2%)
    pallas_call x1, Pallas kernels, shards(): pl.pallas_call(functools.partial(kernel, n_rows, n_x, n_feat), out_shape=...  37.8 us

profile of v4, /device:TPU:0, one launch (start us, length us, event | category | flops | bytes accessed | tf_op | source)
XLA Modules:
  0.0 38.4 jit_solution(13001037639951209018)
XLA Ops:
  0.0 37.8 %shard_map.46 = f32[4,4,63]{2,1,0:T(4,128)S(1)} custom-call(f32[64,4096]{1,0:T(8,128)} %bitcast.3, s32[256,128]{1,0:T(8,128)} %bitcast.4, s32[32,32768]{1,0:T(8,128)} %bins_hbm.1, s32[4,64]{1,0:T(4,128)} %bitcast.5), custom_call_target="tpu_custom_call" | custom-call | tf_op jit(solution)/shard_map/pallas_call | solution.py:343
  37.8 0.6 %copy.6 = f32[4,4,63]{2,1,0:T(4,128)} copy(f32[4,4,63]{2,1,0:T(4,128)S(1)} %shard_map.46) | data formatting | bytes 8064

commit v5 on v4

--- a/solution.py
+++ b/solution.py
@@ -257,15 +257,15 @@
     receive(UNITS - 1)
     add_unit(UNITS - 1, last=True)
 
-    def exchange(pair, dist_z, dist_x):
+    def exchange(dist_z, dist_x):
         to_z, to_x = lax.rem(z + dist_z, n_z), lax.rem(x + dist_x, n_x)
         peer = to_z * n_x + to_x
         slot = dist_z * n_x + dist_x
         return pltpu.make_async_remote_copy(
-            src_ref=sbuf.at[pair, peer],
-            dst_ref=rbuf.at[pair, slot],
-            send_sem=send2_sem.at[pair * n_rows + slot],
-            recv_sem=recv2_sem.at[pair * n_rows + slot],
+            src_ref=sbuf.at[peer],
+            dst_ref=rbuf.at[slot],
+            send_sem=send2_sem.at[slot],
+            recv_sem=recv2_sem.at[slot],
             device_id=(peer, feat),
             device_id_type=MESH,
         )
@@ -273,25 +273,22 @@
     dists = [(dist_z, dist_x) for dist_z in range(n_z) for dist_x in range(n_x)][1:]
     dists.sort(key=lambda d: -min(d[0], n_z - d[0]) - min(d[1], n_x - d[1]))
 
-    pl.semaphore_wait(all_in, n_x - 1)
     for pair in range(n_elect // 2):
         folded = [picked[e] + pltpu.roll(picked[e], BINS, 1) for e in (2 * pair, 2 * pair + 1)]
         both = jnp.where(lane_ids < BINS, folded[0], folded[1])
+        columns = slice(pair * LANES, (pair + 1) * LANES)
         for owner in range(n_rows):
-            sbuf[pair, owner, 0:own] = both[owner * own : (owner + 1) * own]
-            sbuf[pair, owner, own : 2 * own] = both[
+            sbuf[owner, 0:own, columns] = both[owner * own : (owner + 1) * own]
+            sbuf[owner, own : 2 * own, columns] = both[
                 classes + owner * own : classes + (owner + 1) * own
             ]
-        for dist in dists:
-            exchange(pair, *dist).start()
-    totals = []
-    for pair in range(n_elect // 2):
-        total = sbuf[pair, row]
-        for dist in reversed(dists):
-            exchange(pair, *dist).wait_recv()
-            total += rbuf[pair, dist[0] * n_x + dist[1]]
-        totals.append(total)
-    total = jnp.concatenate(totals, axis=1)
+    pl.semaphore_wait(all_in, n_x - 1)
+    for dist in dists:
+        exchange(*dist).start()
+    total = sbuf[row]
+    for dist in reversed(dists):
+        exchange(*dist).wait_recv()
+        total += rbuf[dist[0] * n_x + dist[1]]
 
     width = n_elect * BINS
     bin_of = lax.rem(lax.broadcasted_iota(jnp.int32, total.shape, 1), BINS)
@@ -326,9 +323,8 @@
         copy.wait_send()
     for slot in range(12, 28):
         send(feat, 0, other, slot, 0).wait_send()
-    for pair in range(n_elect // 2):
-        for dist in dists:
-            exchange(pair, *dist).wait_send()
+    for dist in dists:
+        exchange(*dist).wait_send()
 
 
 def shards(scores, labels, bins, elected):
@@ -355,13 +351,13 @@
             pltpu.VMEM((2 * classes, fgrp * BINS), f32),
             pltpu.VMEM((n_elect, 2 * classes, LANES), f32),
             pltpu.VMEM((n_elect, 2 * classes, LANES), f32),
-            pltpu.VMEM((n_elect // 2, n_rows, 2 * own, LANES), f32),
-            pltpu.VMEM((n_elect // 2, n_rows, 2 * own, LANES), f32),
+            pltpu.VMEM((n_rows, 2 * own, n_elect * BINS), f32),
+            pltpu.VMEM((n_rows, 2 * own, n_elect * BINS), f32),
             dma((7,)),
             dma((28,)),
             dma((PIECES,)),
-            dma((n_elect // 2 * n_rows,)),
-            dma((n_elect // 2 * n_rows,)),
+            dma((n_rows,)),
+            dma((n_rows,)),
             pltpu.SemaphoreType.REGULAR,
         ],
         compiler_params=pltpu.CompilerParams(

time: 38.8 us -> 38.3 us (0.987)
  Pallas kernels: 37.8 us -> 37.3 us
    pallas_call x1, Pallas kernels: 37.8 us -> 37.3 us  [shards(): pl.pallas_call(functools.partial(kernel, n_rows, n_x, n_feat), out_shape=...]
where the time goes in v5:
time: 38.3 us; the launch traced here: 37.9 us
  Pallas kernels  37.3 us (97%)
  local copies, waits for them, and re-layouts  0.6 us (2%)
    pallas_call x1, Pallas kernels, shards(): pl.pallas_call(functools.partial(kernel, n_rows, n_x, n_feat), out_shape=...  37.3 us

profile of v5, /device:TPU:0, one launch (start us, length us, event | category | flops | bytes accessed | tf_op | source)
XLA Modules:
  0.0 37.9 jit_solution(18411650297715974765)
XLA Ops:
  0.0 37.3 %shard_map.46 = f32[4,4,63]{2,1,0:T(4,128)S(1)} custom-call(f32[64,4096]{1,0:T(8,128)} %bitcast.3, s32[256,128]{1,0:T(8,128)} %bitcast.4, s32[32,32768]{1,0:T(8,128)} %bins_hbm.1, s32[4,64]{1,0:T(4,128)} %bitcast.5), custom_call_target="tpu_custom_call" | custom-call | tf_op jit(solution)/shard_map/pallas_call | solution.py:339
  37.3 0.6 %copy.6 = f32[4,4,63]{2,1,0:T(4,128)} copy(f32[4,4,63]{2,1,0:T(4,128)S(1)} %shard_map.46) | data formatting | bytes 8064
